TPU v7x, 256 devices: a whole 4x4x8 slice. The times are simulated.
256 devices in a mesh: group: 8 (over y, core), dev: 32 (over z, x).
Axes of the slice: x: 4, y: 4, z: 8, core: 2. Of those that a mesh axis runs over, the one named last changes fastest.
Arguments:
- points: float32 [440, 131072], P(None, ('group', 'dev')), may hold values from -6 to 6
- residual: float32 [147, 131072], P(None, ('group', 'dev')), may hold values from -6 to 6
- coeffs: float32 [147, 131072], P(None, ('group', 'dev')), may hold values from -3 to 3
- owners: int32 [2], replicated, may hold values from 0 to 255
- offsets: int32 [2], replicated, may hold values from 0 to 256
Outputs:
- new_residual: float32 [147, 131072], P(None, ('group', 'dev'))
- new_coeffs: float32 [147, 131072], P(None, ('group', 'dev'))
All inputs are finite; a program needn't handle non-finite values.
Results may differ from a plain program's by a relative error of at most 0.0003.
Values sent between devices are 32-bit elements; how exact they have to be, the bound alone decides.
No kernel may reach another device: no remote copies, remote signals or barrier semaphores. Data moves between devices by JAX's collectives and lax.ppermute only.
A program may use at most 64 MiB of HBM per device.

v0:
```python
import jax
import jax.numpy as jnp
from jax import lax
from jax.sharding import PartitionSpec as P

BLOCK = 256
ridge = 2.0
step_norm = 1.5


def spread_2(value, axis, root):
    mine = lax.axis_index(axis) == root
    return lax.psum(jnp.where(mine, value, jnp.zeros_like(value)), axis)


def kernel_tile(cols, block):
    cross = lax.dot_general(
        block,
        cols,
        (((0,), (0,)), ((), ())),
        precision=lax.Precision.HIGHEST,
        preferred_element_type=jnp.float32,
    )
    dist = (
        jnp.sum(block * block, axis=0)[:, None]
        + jnp.sum(cols * cols, axis=0)[None, :]
        - 2.0 * cross
    )
    return jnp.exp(-dist / cols.shape[0])


def precondition(grad, block):
    gram = kernel_tile(block, block) + ridge * jnp.eye(block.shape[1], dtype=jnp.float32)
    lower = jnp.linalg.cholesky(gram)
    inner = lax.linalg.triangular_solve(lower, grad.T, left_side=True, lower=True)
    solved = lax.linalg.triangular_solve(lower, inner, left_side=True, lower=True, transpose_a=True)
    scale = step_norm / jnp.sqrt(jnp.mean(grad * grad) + 1e-06)
    return scale * solved.T


def contract(left, right):
    return lax.dot_general(
        left,
        right,
        (((1,), (1,)), ((), ())),
        precision=lax.Precision.HIGHEST,
        preferred_element_type=jnp.float32,
    )


def spread(delta, tile):
    return jnp.dot(delta, tile, precision=lax.Precision.HIGHEST, preferred_element_type=jnp.float32)


def body(points, residual, coeffs, owners, offsets):
    here = lax.axis_index(("group", "dev"))
    for step in range(2):
        local = lax.dynamic_slice_in_dim(points, offsets[step], BLOCK, 1)
        block = spread_2(local, ("group", "dev"), owners[step])
        tile = kernel_tile(points, block)
        grad = lax.psum(contract(residual, tile), ("group", "dev"))
        delta = precondition(grad, block)
        residual = residual - spread(delta, tile)
        current = lax.dynamic_slice_in_dim(coeffs, offsets[step], BLOCK, 1)
        mine = jnp.where(here == owners[step], delta, jnp.zeros_like(delta))
        coeffs = lax.dynamic_update_slice_in_dim(coeffs, current + mine, offsets[step], 1)
    return (residual, coeffs)


def solution(mesh):
    return jax.shard_map(
        body,
        mesh=mesh,
        in_specs=(
            P(None, ("group", "dev")),
            P(None, ("group", "dev")),
            P(None, ("group", "dev")),
            P(),
            P(),
        ),
        out_specs=(P(None, ("group", "dev")), P(None, ("group", "dev"))),
        check_vma=False,
    )
```

profile of v0, /device:TPU:1, one launch (start us, length us, event | category | flops | bytes accessed | tf_op | source)
XLA Modules:
  0.0 847.5 jit_solution(16834892905847499718)
XLA Ops:
  7.2 1.0 copy.40
  15.9 2.6 dynamic-slice_select_fusion
  18.7 256.7 %all-reduce.6.cloned.1.call-done = f32[440,256]{1,0:T(8,128)} async-done(((f32[440,256]{1,0:T(8,128)}), f32[440,256]{1,0:T(8,128)}) %all-reduce.6.cloned.1.call-update) | async-done | bytes 450576 | tf_op jit(solution)/shard_map/psum | solution.py:13
  275.4 1.2 multiply_reduce_fusion.2
  276.6 1.0 fusion.12
  277.8 11.7 %cholesky.130 = f32[128,128]{1,0:T(8,128)S(1)} custom-call(f32[128,128]{1,0:T(8,128)S(1)} %cholesky.194), custom_call_target="Cholesky" | custom-call | tf_op jit(solution)/shard_map/jit(cholesky)/cholesky | solution.py:34
  289.6 9.8 %custom-call.17 = f32[1,128,128]{1,2,0:T(8,128)S(1)} custom-call(f32[1,128,128]{2,1,0:T(8,128)S(1)} %get-tuple-element.68), custom_call_target="InvertDiagBlocksLowerTriangular" | custom-call | tf_op jit(solution)/shard_map/jit(cholesky)/cholesky | solution.py:34
  299.9 11.7 %cholesky.147 = f32[128,128]{1,0:T(8,128)S(1)} custom-call(f32[128,128]{1,0:T(8,128)S(1)} %convolution_subtract_fusion.7), custom_call_target="Cholesky" | custom-call | tf_op jit(solution)/shard_map/jit(cholesky)/cholesky | solution.py:34
  311.6 12.0 %fusion.7 = f32[256,512]{1,0:T(8,128)S(1)} fusion(f32[440,256]{1,0:T(8,128)S(1)} %copy-done.2, f32[440,512]{1,0:T(8,128)S(1)} %copy-done, f32[512]{0:T(512)S(1)} %multiply_reduce_fusion, f32[256]{0:T(256)S(1)} %multiply_reduce_fusion.2), kind=kOutput, calls=%fused_computation.13 | convolution fusion | flops 692715520 | bytes 1879040 | tf_op jit(solution)/shard_map/dot_general | solution.py:17
  323.7 1.3 convolution_bitcast_fusion
  327.2 4.0 while.8
  327.8 1.4 bitcast_dynamic-update-slice_fusion.4
  329.8 1.4 bitcast_dynamic-update-slice_fusion.4
  331.2 19.7 %custom-call.19 = f32[2,128,128]{1,2,0:T(8,128)S(1)} custom-call(f32[2,128,128]{2,1,0:T(8,128)S(1)} %get-tuple-element.34), custom_call_target="InvertDiagBlocksLowerTriangular" | custom-call | tf_op jit(solution)/shard_map/triangular_solve/custom-call.4 | solution.py:36
  350.9 226.4 %all-reduce.10.cloned.1.call-done = (f32[147,256]{1,0:T(8,128)}, f32[440,256]{1,0:T(8,128)}) async-done(((f32[147,256]{1,0:T(8,128)}, f32[440,256]{1,0:T(8,128)}), (f32[147,256]{1,0:T(8,128)}, f32[440,256]{1,0:T(8,128)})) %all-reduce.10.cloned.1.call-update) | async-done | bytes 601104 | tf_op jit(solution)/shard_map/psum | solution.py:61
  577.3 1.2 multiply_reduce_fusion.1
  578.5 1.2 fusion.5
  579.7 1.0 fusion.17
  584.3 1.4 fusion.48
  585.8 11.7 %cholesky.164 = f32[128,128]{1,0:T(8,128)S(1)} custom-call(f32[128,128]{1,0:T(8,128)S(1)} %cholesky.197), custom_call_target="Cholesky" | custom-call | tf_op jit(solution)/shard_map/jit(cholesky)/cholesky | solution.py:34
  597.6 9.8 %custom-call.20 = f32[1,128,128]{1,2,0:T(8,128)S(1)} custom-call(f32[1,128,128]{2,1,0:T(8,128)S(1)} %get-tuple-element.64), custom_call_target="InvertDiagBlocksLowerTriangular" | custom-call | tf_op jit(solution)/shard_map/jit(cholesky)/cholesky | solution.py:34
  607.9 11.9 %cholesky.181 = f32[128,128]{1,0:T(8,128)S(1)} custom-call(f32[128,128]{1,0:T(8,128)S(1)} %convolution_subtract_fusion.6), custom_call_target="Cholesky" | custom-call | tf_op jit(solution)/shard_map/jit(cholesky)/cholesky | solution.py:34
  621.9 4.0 while.9
  622.5 1.4 bitcast_dynamic-update-slice_fusion.5
  624.4 1.4 bitcast_dynamic-update-slice_fusion.5
  625.8 19.7 %custom-call.22 = f32[2,128,128]{1,2,0:T(8,128)S(1)} custom-call(f32[2,128,128]{2,1,0:T(8,128)S(1)} %get-tuple-element.36), custom_call_target="InvertDiagBlocksLowerTriangular" | custom-call | tf_op jit(solution)/shard_map/triangular_solve/custom-call.4 | solution.py:36
  645.6 1.5 dynamic_update_slice.6
  647.1 185.8 %all-reduce.8.cloned.1.call-done = f32[147,256]{1,0:T(8,128)} async-done(((f32[147,256]{1,0:T(8,128)}), f32[147,256]{1,0:T(8,128)}) %all-reduce.8.cloned.1.call-update) | async-done | bytes 150544 | tf_op jit(solution)/shard_map/psum | solution.py:61
  832.9 1.2 fusion.20
  837.0 1.2 convolution_subtract_fusion
  838.3 1.5 dynamic_update_slice.7
  839.8 0.7 copy-done.4
  (74 shorter events, 13.4 us)
Async XLA Ops:
  7.2 268.3 %all-reduce.6.cloned.1.call-start = ((), (), s32[]{:S(2)}) async-start(), calls=%async_computation | async-start | bytes 901120 | tf_op jit(solution)/shard_map/psum | solution.py:13
  8.2 0.7 copy-start.7
  12.0 0.7 copy-start.8
  15.9 2.7 copy-start
  18.5 558.8 %all-reduce.10.cloned.1.call-start = ((), (), s32[]{:S(2)}) async-start(), calls=%async_computation.2 | async-start | bytes 1212416 | tf_op jit(solution)/shard_map/psum | solution.py:61
  275.4 1.2 copy-start.2
  311.6 12.0 %copy-start.3 = (f32[147,512]{1,0:T(8,128)S(1)}, f32[147,512]{1,0:T(8,128)}, u32[]{:S(2)}) copy-start(f32[147,512]{1,0:T(8,128)} %param.11) | copy-start | bytes 903172
  325.0 507.9 %all-reduce.8.cloned.1.call-start = ((), (), s32[]{:S(2)}) async-start(), calls=%async_computation.1 | async-start | bytes 311296 | tf_op jit(solution)/shard_map/psum | solution.py:61
  577.3 1.2 copy-start.1
  579.6 1.0 copy-start.6
  832.9 1.2 copy-start.5
  839.8 0.7 copy-start.4
Sparse Core Ops, SparseCore 0:
  18.7 256.7 all-reduce.5
  325.1 252.1 all-reduce.9
  585.8 247.1 all-reduce.7
where the time goes:
time: 857 us; the launch traced here: 847 us
  waiting for transfers between devices  669 us (78%)
  other arithmetic  114 us (13%)
  matrix products  24.9 us (3%)
  between operations  23.6 us (3%)
  local copies, waits for them, and re-layouts  15.5 us (2%)
    psum x2, waiting for transfers between devices, body(): grad = lax.psum(contract(residual, tile), ('group', 'dev'))  412 us
    psum x1, waiting for transfers between devices, spread_2(): return lax.psum(jnp.where(mine, value, jnp.zeros_like(value)), axis)  257 us
    another operation x12, other arithmetic, precondition(): lower = jnp.linalg.cholesky(gram)  68.2 us
    another operation x5, other arithmetic, precondition(): lax.linalg.triangular_solve(lower, inner, left_side=True, lower=True, tra...  39.4 us
  transfers between devices with their start and end apart: 3, of which 3 were waited for; matrix products, arithmetic and copies ran while one was open for 10% of the time, Pallas kernels for 0%

commit v1 on v0

--- a/solution.py
+++ b/solution.py
@@ -58,7 +58,7 @@
         local = lax.dynamic_slice_in_dim(points, offsets[step], BLOCK, 1)
         block = spread_2(local, ("group", "dev"), owners[step])
         tile = kernel_tile(points, block)
-        grad = lax.psum(contract(residual, tile), ("group", "dev"))
+        grad = lax.psum(lax.psum(contract(residual, tile), "dev"), "group")
         delta = precondition(grad, block)
         residual = residual - spread(delta, tile)
         current = lax.dynamic_slice_in_dim(coeffs, offsets[step], BLOCK, 1)

time: 857 us -> 720 us (0.84)
  waiting for transfers between devices: 669 us -> 544 us
  matrix products: 24.9 us -> 15.3 us
    psum x2 -> x4, waiting for transfers between devices: 412 us -> 285 us  [body(): grad = lax.psum(lax.psum(contract(residual, tile), 'dev'), 'group')]
    dot_general x4, matrix products: 15.2 us -> 4.62 us  [kernel_tile(): lax.dot_general(block, cols, (((0,), (0,)), ((), ())), precision=lax.Prec...]
  transfers between devices with their start and end apart: 3 -> 5, of which waited for: 3 -> 5; matrix products, arithmetic and copies ran while one was open for 10% -> 17% of each run, Pallas kernels for 0% -> 0%
where the time goes in v1:
time: 720 us; the launch traced here: 716 us
  waiting for transfers between devices  544 us (76%)
  other arithmetic  114 us (16%)
  between operations  23.5 us (3%)
  local copies, waits for them, and re-layouts  18.6 us (3%)
  matrix products  15.3 us (2%)
    psum x4, waiting for transfers between devices, body(): grad = lax.psum(lax.psum(contract(residual, tile), 'dev'), 'group')  285 us
    psum x1, waiting for transfers between devices, spread_2(): return lax.psum(jnp.where(mine, value, jnp.zeros_like(value)), axis)  259 us
    another operation x12, other arithmetic, precondition(): lower = jnp.linalg.cholesky(gram)  68 us
    another operation x5, other arithmetic, precondition(): lax.linalg.triangular_solve(lower, inner, left_side=True, lower=True, tra...  40.2 us
  transfers between devices with their start and end apart: 5, of which 5 were waited for; matrix products, arithmetic and copies ran while one was open for 17% of the time, Pallas kernels for 0%

profile of v1, /device:TPU:1, one launch (start us, length us, event | category | flops | bytes accessed | tf_op | source)
XLA Modules:
  0.0 716.2 jit_solution(139602668222635119)
XLA Ops:
  15.9 2.6 dynamic-slice_select_fusion
  18.5 1.1 copy-done
  19.7 259.5 %all-reduce.16.cloned.1.call-done = (f32[440,256]{1,0:T(8,128)}, f32[440,256]{1,0:T(8,128)}) async-done(((f32[440,256]{1,0:T(8,128)}, f32[440,256]{1,0:T(8,128)}), (f32[440,256]{1,0:T(8,128)}, f32[440,256]{1,0:T(8,128)})) %all-reduce.16.cloned.1.call-update) | async-done | bytes 901136 | tf_op jit(solution)/shard_map/psum | solution.py:13
  279.2 1.2 multiply_reduce_fusion.2
  281.4 1.2 fusion.7
  282.6 1.3 convolution_bitcast_fusion
  284.7 11.7 %cholesky.130 = f32[128,128]{1,0:T(8,128)S(1)} custom-call(f32[128,128]{1,0:T(8,128)S(1)} %cholesky.194), custom_call_target="Cholesky" | custom-call | tf_op jit(solution)/shard_map/jit(cholesky)/cholesky | solution.py:34
  296.5 9.8 %custom-call.17 = f32[1,128,128]{1,2,0:T(8,128)S(1)} custom-call(f32[1,128,128]{2,1,0:T(8,128)S(1)} %get-tuple-element.68), custom_call_target="InvertDiagBlocksLowerTriangular" | custom-call | tf_op jit(solution)/shard_map/jit(cholesky)/cholesky | solution.py:34
  306.8 11.7 %cholesky.147 = f32[128,128]{1,0:T(8,128)S(1)} custom-call(f32[128,128]{1,0:T(8,128)S(1)} %convolution_subtract_fusion.7), custom_call_target="Cholesky" | custom-call | tf_op jit(solution)/shard_map/jit(cholesky)/cholesky | solution.py:34
  320.6 4.2 while.8
  321.3 1.3 bitcast_dynamic-update-slice_fusion.4
  323.3 1.3 bitcast_dynamic-update-slice_fusion.4
  325.5 1.0 fusion.17
  327.5 11.7 %cholesky.164 = f32[128,128]{1,0:T(8,128)S(1)} custom-call(f32[128,128]{1,0:T(8,128)S(1)} %cholesky.197), custom_call_target="Cholesky" | custom-call | tf_op jit(solution)/shard_map/jit(cholesky)/cholesky | solution.py:34
  339.2 9.8 %custom-call.20 = f32[1,128,128]{1,2,0:T(8,128)S(1)} custom-call(f32[1,128,128]{2,1,0:T(8,128)S(1)} %get-tuple-element.64), custom_call_target="InvertDiagBlocksLowerTriangular" | custom-call | tf_op jit(solution)/shard_map/jit(cholesky)/cholesky | solution.py:34
  349.5 11.7 %cholesky.181 = f32[128,128]{1,0:T(8,128)S(1)} custom-call(f32[128,128]{1,0:T(8,128)S(1)} %convolution_subtract_fusion.6), custom_call_target="Cholesky" | custom-call | tf_op jit(solution)/shard_map/jit(cholesky)/cholesky | solution.py:34
  363.4 1.4 fusion.5
  364.8 57.1 %all-reduce.8.cloned.1.call-done = f32[147,256]{1,0:T(8,128)} async-done(((f32[147,256]{1,0:T(8,128)}), f32[147,256]{1,0:T(8,128)}) %all-reduce.8.cloned.1.call-update) | async-done | bytes 150544 | tf_op jit(solution)/shard_map/psum | solution.py:61
  422.0 20.5 %custom-call.19 = f32[2,128,128]{1,2,0:T(8,128)S(1)} custom-call(f32[2,128,128]{2,1,0:T(8,128)} %copy-done.9), custom_call_target="InvertDiagBlocksLowerTriangular" | custom-call | tf_op jit(solution)/shard_map/triangular_solve/custom-call.4 | solution.py:36
  442.5 47.3 %all-reduce.10.cloned.1.call-done = f32[147,256]{1,0:T(8,128)} async-done(((f32[147,256]{1,0:T(8,128)}), f32[147,256]{1,0:T(8,128)}) %all-reduce.10.cloned.1.call-update) | async-done | bytes 150544 | tf_op jit(solution)/shard_map/psum | solution.py:61
  489.8 1.2 fusion.22
  494.3 1.4 fusion.48
  496.4 3.9 while.9
  497.0 1.4 bitcast_dynamic-update-slice_fusion.5
  498.9 1.4 bitcast_dynamic-update-slice_fusion.5
  500.3 19.7 %custom-call.22 = f32[2,128,128]{1,2,0:T(8,128)S(1)} custom-call(f32[2,128,128]{2,1,0:T(8,128)S(1)} %get-tuple-element.36), custom_call_target="InvertDiagBlocksLowerTriangular" | custom-call | tf_op jit(solution)/shard_map/triangular_solve/custom-call.4 | solution.py:36
  520.0 114.1 %all-reduce.12.cloned.1.call-done = f32[147,256]{1,0:T(8,128)} async-done(((f32[147,256]{1,0:T(8,128)}), f32[147,256]{1,0:T(8,128)}) %all-reduce.12.cloned.1.call-update) | async-done | bytes 150544 | tf_op jit(solution)/shard_map/psum | solution.py:61
  634.2 1.5 dynamic_update_slice.6
  635.7 66.1 %all-reduce.14.cloned.1.call-done = f32[147,256]{1,0:T(8,128)} async-done(((f32[147,256]{1,0:T(8,128)}), f32[147,256]{1,0:T(8,128)}) %all-reduce.14.cloned.1.call-update) | async-done | bytes 150544 | tf_op jit(solution)/shard_map/psum | solution.py:61
  701.8 1.2 fusion.20
  705.9 1.2 convolution_subtract_fusion
  707.2 1.5 dynamic_update_slice.7
  (90 shorter events, 18.5 us)
Async XLA Ops:
  7.2 272.0 %all-reduce.16.cloned.1.call-start = ((), (), s32[]{:S(2)}) async-start(), calls=%async_computation.4 | async-start | bytes 1802240 | tf_op jit(solution)/shard_map/psum | solution.py:13
  8.2 0.7 copy-start.10
  12.0 0.7 copy-start.11
  18.5 1.2 copy-start
  18.5 403.4 %all-reduce.8.cloned.1.call-start = ((), (), s32[]{:S(2)}) async-start(), calls=%async_computation | async-start | bytes 311296 | tf_op jit(solution)/shard_map/psum | solution.py:61
  279.2 1.2 copy-start.2
  281.4 1.2 copy-start.3
  284.0 205.8 %all-reduce.10.cloned.1.call-start = ((), (), s32[]{:S(2)}) async-start(), calls=%async_computation.1 | async-start | bytes 311296 | tf_op jit(solution)/shard_map/psum | solution.py:61
  320.5 5.0 copy-start.1
  324.8 0.6 copy-start.9
  324.8 0.7 copy-start.12
  326.7 0.7 copy-start.5
  327.5 21.6 %copy-start.6 = (f32[256,256]{1,0:T(8,128)S(1)}, f32[256,256]{1,0:T(8,128)}, u32[]{:S(2)}) copy-start(f32[256,256]{1,0:T(8,128)} %copy-done.5) | copy-start | bytes 786436
  421.9 212.1 %all-reduce.12.cloned.1.call-start = ((), (), s32[]{:S(2)}) async-start(), calls=%async_computation.2 | async-start | bytes 311296 | tf_op jit(solution)/shard_map/psum | solution.py:61
  489.8 1.2 copy-start.7
  495.7 0.7 copy-start.13
  495.7 206.1 %all-reduce.14.cloned.1.call-start = ((), (), s32[]{:S(2)}) async-start(), calls=%async_computation.3 | async-start | bytes 311296 | tf_op jit(solution)/shard_map/psum | solution.py:61
  701.8 1.2 copy-start.8
  708.7 0.7 copy-start.4
Sparse Core Ops, SparseCore 0:
  18.6 260.5 all-reduce.15
  284.1 137.7 all-reduce.7
  424.3 65.4 all-reduce.9
  495.8 138.1 all-reduce.11
  636.3 65.5 all-reduce.13

commit v2 on v0

--- a/solution.py
+++ b/solution.py
@@ -58,7 +58,7 @@
         local = lax.dynamic_slice_in_dim(points, offsets[step], BLOCK, 1)
         block = spread_2(local, ("group", "dev"), owners[step])
         tile = kernel_tile(points, block)
-        grad = lax.psum(contract(residual, tile), ("group", "dev"))
+        grad = jnp.sum(lax.all_gather(contract(residual, tile), ("group", "dev")), axis=0)
         delta = precondition(grad, block)
         residual = residual - spread(delta, tile)
         current = lax.dynamic_slice_in_dim(coeffs, offsets[step], BLOCK, 1)

time: 857 us -> 658 us (0.77)
  waiting for transfers between devices: 669 us -> 444 us
  other arithmetic: 114 us -> 143 us
  loops' own time: 0.1 us -> 11.2 us
    psum x2 -> x0, waiting for transfers between devices: 412 us -> none  [body(): grad = lax.psum(contract(residual, tile), ('group', 'dev'))]
    all_gather x0 -> x2, waiting for transfers between devices: none -> 184 us  [body(): lax.all_gather(contract(residual, tile), ('group', 'dev'))]
    reduce_sum x0 -> x2, other arithmetic: none -> 27.9 us  [body(): jnp.sum(lax.all_gather(contract(residual, tile), ('group', 'dev')), axis=0)]
    another operation x2, loops' own time: 0.1 us -> 11.2 us  [precondition(): lax.linalg.triangular_solve(lower, inner, left_side=True, lower=True, tra...]
  transfers between devices with their start and end apart: 3 -> 3, of which waited for: 3 -> 3; matrix products, arithmetic and copies ran while one was open for 10% -> 19% of each run, Pallas kernels for 0% -> 0%
where the time goes in v2:
time: 658 us; the launch traced here: 655 us
  waiting for transfers between devices  444 us (67%)
  other arithmetic  143 us (22%)
  between operations  23.2 us (4%)
  matrix products  18 us (3%)
  local copies, waits for them, and re-layouts  15.3 us (2%)
  loops' own time  11.2 us (2%)
    psum x1, waiting for transfers between devices, spread_2(): return lax.psum(jnp.where(mine, value, jnp.zeros_like(value)), axis)  259 us
    all_gather x2, waiting for transfers between devices, body(): lax.all_gather(contract(residual, tile), ('group', 'dev'))  184 us
    another operation x12, other arithmetic, precondition(): lower = jnp.linalg.cholesky(gram)  68.1 us
    another operation x5, other arithmetic, precondition(): lax.linalg.triangular_solve(lower, inner, left_side=True, lower=True, tra...  39.4 us
    reduce_sum x2, other arithmetic, body(): jnp.sum(lax.all_gather(contract(residual, tile), ('group', 'dev')), axis=0)  27.9 us
  transfers between devices with their start and end apart: 3, of which 3 were waited for; matrix products, arithmetic and copies ran while one was open for 19% of the time, Pallas kernels for 0%

profile of v2, /device:TPU:1, one launch (start us, length us, event | category | flops | bytes accessed | tf_op | source)
XLA Modules:
  0.0 655.1 jit_solution(14946706453486705296)
XLA Ops:
  8.2 1.3 fusion.47
  12.1 1.4 fusion.46
  16.1 2.6 dynamic-slice_select_fusion
  18.7 1.3 multiply_reduce_fusion
  20.0 259.4 %all-reduce.4.cloned.1.call-done = (f32[440,256]{1,0:T(8,128)}, f32[440,256]{1,0:T(8,128)}) async-done(((f32[440,256]{1,0:T(8,128)}, f32[440,256]{1,0:T(8,128)}), (f32[440,256]{1,0:T(8,128)}, f32[440,256]{1,0:T(8,128)})) %all-reduce.4.cloned.1.call-update) | async-done | bytes 901136 | tf_op jit(solution)/shard_map/psum | solution.py:13
  279.4 1.1 multiply_reduce_fusion.2
  280.5 2.5 fusion.7
  283.0 2.3 convolution_bitcast_fusion.1
  285.8 2.3 fusion.12
  288.2 11.7 %cholesky.130 = f32[128,128]{1,0:T(8,128)S(1)} custom-call(f32[128,128]{1,0:T(8,128)S(1)} %cholesky.194), custom_call_target="Cholesky" | custom-call | tf_op jit(solution)/shard_map/jit(cholesky)/cholesky | solution.py:34
  300.0 9.8 %custom-call.17 = f32[1,128,128]{1,2,0:T(8,128)S(1)} custom-call(f32[1,128,128]{2,1,0:T(8,128)S(1)} %get-tuple-element.68), custom_call_target="InvertDiagBlocksLowerTriangular" | custom-call | tf_op jit(solution)/shard_map/jit(cholesky)/cholesky | solution.py:34
  310.3 11.7 %cholesky.147 = f32[128,128]{1,0:T(8,128)S(1)} custom-call(f32[128,128]{1,0:T(8,128)S(1)} %convolution_subtract_fusion.7), custom_call_target="Cholesky" | custom-call | tf_op jit(solution)/shard_map/jit(cholesky)/cholesky | solution.py:34
  324.0 14.8 %while.8 = (s32[]{:T(128)}, f32[256,256]{1,0:T(8,128)S(1)}, s32[2,2]{1,0:T(2,128)S(1)}, f32[2,128,128]{2,1,0:T(8,128)S(1)}, s32[]{:T(128)}) while((s32[]{:T(128)}, f32[256,256]{1,0:T(8,128)S(1)}, s32[2,2]{1,0:T(2,128)S(1)}, f32[2,128,128]{2,1,0:T(8,128)S(1)}, s32[]{:T(128)}) %tuple.59), condition=%wide.while_cond.1, body=%wide.while_body.1.sunk | while | flops 2 | bytes 131189 | solution.py:36
  335.7 1.3 bitcast_dynamic-update-slice_fusion.4
  337.6 1.3 bitcast_dynamic-update-slice_fusion.4
  338.9 19.7 %custom-call.19 = f32[2,128,128]{1,2,0:T(8,128)S(1)} custom-call(f32[2,128,128]{2,1,0:T(8,128)S(1)} %get-tuple-element.34), custom_call_target="InvertDiagBlocksLowerTriangular" | custom-call | tf_op jit(solution)/shard_map/triangular_solve/custom-call.4 | solution.py:36
  359.7 2.5 fusion.5
  362.1 85.6 %all-gather.7.cloned.1.call-done = f32[256,147,256]{2,1,0:T(8,128)} async-done(((f32[1,147,256]{2,1,0:T(8,128)}), f32[256,147,256]{2,1,0:T(8,128)}) %all-gather.7.cloned.1.call-update) | async-done | bytes 38535184 | tf_op jit(solution)/shard_map/all_gather | solution.py:61
  447.8 14.0 %reduce_sum.64 = f32[147,256]{1,0:T(8,128)S(1)} reduce(f32[256,147,256]{2,1,0:T(8,128)} %all-gather.7.cloned.1.call-done, f32[]{:T(128)} %constant.93.clone.1), dimensions={0}, to_apply=%region_3.4 | reduce | flops 9596160 | bytes 38685700 | tf_op jit(solution)/shard_map/reduce_sum | solution.py:61
  465.3 1.4 convolution_bitcast_fusion
  468.0 11.7 %cholesky.164 = f32[128,128]{1,0:T(8,128)S(1)} custom-call(f32[128,128]{1,0:T(8,128)S(1)} %cholesky.197), custom_call_target="Cholesky" | custom-call | tf_op jit(solution)/shard_map/jit(cholesky)/cholesky | solution.py:34
  479.7 9.8 %custom-call.20 = f32[1,128,128]{1,2,0:T(8,128)S(1)} custom-call(f32[1,128,128]{2,1,0:T(8,128)S(1)} %get-tuple-element.64), custom_call_target="InvertDiagBlocksLowerTriangular" | custom-call | tf_op jit(solution)/shard_map/jit(cholesky)/cholesky | solution.py:34
  490.0 11.9 %cholesky.181 = f32[128,128]{1,0:T(8,128)S(1)} custom-call(f32[128,128]{1,0:T(8,128)S(1)} %convolution_subtract_fusion.6), custom_call_target="Cholesky" | custom-call | tf_op jit(solution)/shard_map/jit(cholesky)/cholesky | solution.py:34
  503.8 3.8 while.9
  504.4 1.3 bitcast_dynamic-update-slice_fusion.5
  506.3 1.3 bitcast_dynamic-update-slice_fusion.5
  507.6 19.7 %custom-call.22 = f32[2,128,128]{1,2,0:T(8,128)S(1)} custom-call(f32[2,128,128]{2,1,0:T(8,128)S(1)} %get-tuple-element.36), custom_call_target="InvertDiagBlocksLowerTriangular" | custom-call | tf_op jit(solution)/shard_map/triangular_solve/custom-call.4 | solution.py:36
  527.4 1.5 dynamic_update_slice.6
  528.9 98.8 %all-gather.9.cloned.1.call-done = f32[256,147,256]{2,1,0:T(8,128)} async-done(((f32[1,147,256]{2,1,0:T(8,128)}), f32[256,147,256]{2,1,0:T(8,128)}) %all-gather.9.cloned.1.call-update) | async-done | bytes 38535184 | tf_op jit(solution)/shard_map/all_gather | solution.py:61
  627.7 14.0 %reduce_sum.70 = f32[147,256]{1,0:T(8,128)S(1)} reduce(f32[256,147,256]{2,1,0:T(8,128)} %all-gather.9.cloned.1.call-done, f32[]{:T(128)} %constant.93.clone.1), dimensions={0}, to_apply=%region_11.0 | reduce | flops 9596160 | bytes 38685700 | tf_op jit(solution)/shard_map/reduce_sum | solution.py:61
  644.8 1.2 convolution_subtract_fusion
  646.1 1.5 dynamic_update_slice.7
  (64 shorter events, 15.1 us)
Async XLA Ops:
  7.2 457.7 %copy-start.1 = (f32[147,512]{1,0:T(8,128)S(1)}, f32[147,512]{1,0:T(8,128)}, u32[]{:S(2)}) copy-start(f32[147,512]{1,0:T(8,128)} %param.11) | copy-start | bytes 903172
  7.2 272.2 %all-reduce.4.cloned.1.call-start = ((), (), s32[]{:S(2)}) async-start(), calls=%async_computation.2 | async-start | bytes 1802240 | tf_op jit(solution)/shard_map/psum | solution.py:13
  18.7 429.1 %all-gather.7.cloned.1.call-start = ((), (), s32[]{:S(2)}) async-start(), calls=%async_computation | async-start | bytes 40001536 | tf_op jit(solution)/shard_map/all_gather | solution.py:61
  279.4 187.4 %copy-start = (f32[440,256]{1,0:T(8,128)S(1)}, f32[440,256]{1,0:T(8,128)}, u32[]{:S(2)}) copy-start(f32[440,256]{1,0:T(8,128)} %get-tuple-element.54) | copy-start | bytes 1351684
  285.4 342.4 %all-gather.9.cloned.1.call-start = ((), (), s32[]{:S(2)}) async-start(), calls=%async_computation.1 | async-start | bytes 40001536 | tf_op jit(solution)/shard_map/all_gather | solution.py:61
  647.6 0.7 copy-start.2
Sparse Core Ops, SparseCore 0:
  18.8 260.5 all-reduce.3
  285.5 162.2 all-gather.6
  466.8 160.8 all-gather.8
